TPU v7x, 32 devices: a whole 2x2x4 slice. The times are simulated.
32 devices in a mesh: blk: 8 (over y, x, core), feat: 4 (over z).
Axes of the slice: x: 2, y: 2, z: 4, core: 2. Of those that a mesh axis runs over, the one named last changes fastest.
Arguments:
- features: bfloat16 [128, 8192], P('feat', 'blk'), may hold values from -6 to 6
- weight_in: bfloat16 [128, 256], replicated, may hold values from -0.5 to 0.5
- weight_mid: bfloat16 [256, 256], replicated, may hold values from -0.375 to 0.375
- weight_out: bfloat16 [256, 172], replicated, may hold values from -0.375 to 0.375
- block_values: bfloat16 [8, 8, 16, 128, 128], P('blk'), may hold values from -0.25 to 0.25
- block_dst: int32 [8, 8, 16], P('blk'), may hold values from 0 to 7
- block_src: int32 [8, 8, 16], P('blk'), may hold values from 0 to 7
- block_count: int32 [8, 8], P('blk'), may hold values from 4 to 16, as said below
- labels: int32 [8192], P('blk'), may hold values from 0 to 171
- train_mask: int32 [8192], P('blk'), may hold values from 0 to 1
Outputs:
- loss: float32 [], replicated
- grad_in: float32 [128, 256], P('feat')
- grad_mid: float32 [256, 256], P('feat')
- grad_out: float32 [256, 172], P('feat')
Inputs may be any that keep to these rules, and one draw needn't show every extreme that they name: block_count[b, p] is the number of live slots of the blocks of panel b's rows that read panel p's nodes; block_count[b, b] = 16. Entries of block_dst, block_src and block_values at slots at or past block_count are unused.
All inputs are finite; a program needn't handle non-finite values.
Results may differ from a plain program's by a relative error of at most 0.017.
Values may be sent and summed in bfloat16 or wider, within the bound.
A program may use at most 64 MiB of HBM per device.

v0:
```python
import jax
import jax.numpy as jnp
from jax import lax
from jax.sharding import PartitionSpec as P


def elu(values):
    return jnp.where(values > 0, values, jnp.expm1(values))


def elu_slope(values):
    return jnp.where(values > 0, 1.0, jnp.exp(values))


def panel_folder(values, targets, sources, live_count, breadth, row_blocks, block_size):
    panel_rows = row_blocks * block_size
    slot_index = jnp.arange(values.shape[2], dtype=jnp.int32)

    def folding(running, portion, offset):
        several = portion.shape[1] // panel_rows

        def folding_one_panel(turn_index, accumulated):
            window = lax.dynamic_slice_in_dim(portion, turn_index * panel_rows, panel_rows, 1)
            window = window.reshape(breadth, row_blocks, block_size)
            chosen = jnp.take(window, sources[0, turn_index], axis=1)
            product = jnp.einsum(
                "fsj,sij->fsi", chosen, values[0, turn_index], preferred_element_type=jnp.float32
            )
            live_slots = (slot_index < live_count[0, turn_index]).astype(jnp.float32)
            return accumulated.at[:, targets[0, turn_index]].add(
                product * live_slots[None, :, None]
            )

        return lax.fori_loop(0, several, folding_one_panel, running)

    return folding


def hidden_aggregate(table, values, targets, sources, live_count):
    breadth, panel_rows = table.shape
    block_size = values.shape[-1]
    row_blocks = panel_rows // block_size
    folding = panel_folder(values, targets, sources, live_count, breadth, row_blocks, block_size)
    initial = jnp.zeros((breadth, row_blocks, block_size), jnp.float32)
    summed = folding(initial, lax.all_gather(table, "blk", axis=1, tiled=True), jnp.int32(0))
    return summed.reshape(breadth, panel_rows).astype(jnp.bfloat16)


def spread_back(grads, values, targets, sources, live_count):
    breadth, panel_rows = grads.shape
    block_size = values.shape[-1]
    row_blocks = panel_rows // block_size
    tiles = grads.reshape(breadth, row_blocks, block_size)
    slot_index = jnp.arange(values.shape[2], dtype=jnp.int32)

    def term_one_panel(source_panel):
        chosen = jnp.take(tiles, targets[0, source_panel], axis=1)
        product = jnp.einsum(
            "fsi,sij->fsj", chosen, values[0, source_panel], preferred_element_type=jnp.float32
        )
        live_slots = (slot_index < live_count[0, source_panel]).astype(jnp.float32)
        placed = jnp.zeros((breadth, row_blocks, block_size), jnp.float32)
        placed = placed.at[:, sources[0, source_panel]].add(product * live_slots[None, :, None])
        return placed.reshape(breadth, panel_rows)

    summed = lax.psum_scatter(
        lax.map(term_one_panel, jnp.arange(lax.axis_size("blk") * 1, dtype=jnp.int32)).astype(
            jnp.bfloat16
        ),
        "blk",
        scatter_dimension=0,
        tiled=True,
    ).astype(jnp.float32)
    return summed[0]


def mix_features(weight, table):
    out_part = weight.shape[1] // lax.axis_size("feat")
    position = lax.axis_index("feat")
    own_columns = lax.dynamic_slice_in_dim(weight, position * out_part, out_part, 1)
    return lax.dot_general(
        own_columns,
        lax.all_gather(table, "feat", axis=0, tiled=True),
        (((0,), (0,)), ((), ())),
        preferred_element_type=jnp.float32,
    )


def class_scores(weight_out, table):
    return lax.dot_general(
        weight_out,
        lax.all_gather(table, "feat", axis=0, tiled=True),
        (((0,), (0,)), ((), ())),
        preferred_element_type=jnp.float32,
    )


def weight_columns(gated, own_table, own_weight):
    breadth, panel_rows = own_table.shape
    total_out = gated.shape[0] * lax.axis_size("feat")

    def add_columns(running, portion):
        grad_part = running[0]
        product = lax.dot_general(
            own_table, portion, (((1,), (1,)), ((), ())), preferred_element_type=jnp.float32
        )
        grad_part = product
        if len(running) == 1:
            return (grad_part,)
        return (grad_part, jnp.dot(own_weight, portion, preferred_element_type=jnp.float32))

    grad_zero = jnp.zeros((breadth, total_out), jnp.float32)
    if own_weight is None:
        initial = (grad_zero,)
    else:
        initial = (grad_zero, jnp.zeros((own_weight.shape[0], panel_rows), jnp.float32))
    return add_columns(initial, lax.all_gather(gated, "feat", axis=0, tiled=True))


def shards(
    features,
    weight_in,
    weight_mid,
    weight_out,
    block_values,
    block_dst,
    block_src,
    block_count,
    labels,
    train_mask,
):
    position = lax.axis_index("feat")
    hidden_part = weight_mid.shape[0] // lax.axis_size("feat")
    block_size = block_values.shape[-1]
    in_part, panel_rows = features.shape
    row_blocks = panel_rows // block_size
    folding = panel_folder(
        block_values, block_dst, block_src, block_count, in_part, row_blocks, block_size
    )
    initial = jnp.zeros((in_part, row_blocks, block_size), jnp.float32)
    first_sum = folding(initial, lax.all_gather(features, "blk", axis=1, tiled=True), jnp.int32(0))
    first_agg = first_sum.reshape(in_part, panel_rows).astype(jnp.bfloat16)
    first_pre = mix_features(weight_in, first_agg)
    first_act = elu(first_pre).astype(jnp.bfloat16)
    second_agg = hidden_aggregate(first_act, block_values, block_dst, block_src, block_count)
    second_pre = mix_features(weight_mid, second_agg)
    second_act = elu(second_pre).astype(jnp.bfloat16)
    third_agg = hidden_aggregate(second_act, block_values, block_dst, block_src, block_count)
    out_rows = lax.dynamic_slice_in_dim(weight_out, position * hidden_part, hidden_part, 0)
    logits = class_scores(weight_out, third_agg)
    log_total = jnp.log(jnp.sum(jnp.exp(logits), axis=0))
    one_hot = (jnp.arange(logits.shape[0], dtype=jnp.int32)[:, None] == labels[None, :]).astype(
        jnp.float32
    )
    picked = jnp.sum(one_hot * logits, axis=0)
    weighting = train_mask.astype(jnp.float32)
    loss_total, node_count = lax.psum(
        (jnp.sum(weighting * (log_total - picked)), jnp.sum(weighting)), "blk"
    )
    loss = loss_total / jnp.maximum(node_count, 1.0)
    grad_logits = (weighting[None, :] * (jnp.exp(logits - log_total[None, :]) - one_hot)).astype(
        jnp.bfloat16
    )
    grad_out = lax.dot_general(
        third_agg, grad_logits, (((1,), (1,)), ((), ())), preferred_element_type=jnp.float32
    )
    grad_out = lax.psum(grad_out, "blk")
    third_back = jnp.dot(out_rows, grad_logits, preferred_element_type=jnp.float32).astype(
        jnp.bfloat16
    )
    second_grad = spread_back(third_back, block_values, block_dst, block_src, block_count)
    second_gate = (second_grad * elu_slope(second_pre)).astype(jnp.bfloat16)
    mid_rows = lax.dynamic_slice_in_dim(weight_mid, position * hidden_part, hidden_part, 0)
    grad_mid, second_back = weight_columns(second_gate, second_agg, mid_rows)
    grad_mid = lax.psum(grad_mid, "blk")
    first_grad = spread_back(
        second_back.astype(jnp.bfloat16), block_values, block_dst, block_src, block_count
    )
    first_gate = (first_grad * elu_slope(first_pre)).astype(jnp.bfloat16)
    grad_in = weight_columns(first_gate, first_agg, None)[0]
    grad_in = lax.psum(grad_in, "blk")
    grad_in, grad_mid, grad_out = (grad_in, grad_mid, grad_out)
    return (loss, grad_in, grad_mid, grad_out)


def solution(mesh):
    placed = (
        P("feat", "blk"),
        P(),
        P(),
        P(),
        P("blk", None, None, None, None),
        P("blk", None, None),
        P("blk", None, None),
        P("blk", None),
        P("blk"),
        P("blk"),
    )
    return jax.shard_map(
        shards,
        mesh=mesh,
        in_specs=placed,
        out_specs=(P(), P("feat", None), P("feat", None), P("feat", None)),
        check_vma=False,
    )
```

profile of v0, /device:TPU:0, one launch (start us, length us, event | category | flops | bytes accessed | tf_op | source)
XLA Modules:
  0.0 608.6 jit_solution(1737324306972229232)
XLA Ops:
  7.2 11.6 %all_gather.24 = bf16[32,8192]{1,0:T(8,128)(2,1)S(1)} all-gather(bf16[32,1024]{1,0:T(8,128)(2,1)} %param.22), channel_id=1, replica_groups=mesh['blk'=8,'feat'=4] {'blk'}, dimensions={1}, use_global_device_ids=true | all-gather | bytes 589824 | tf_op jit(solution)/shard_map/all_gather | solution.py:141
  18.9 53.0 %while.64 = (s32[]{:T(128)}, f32[32,8,128]{2,0,1:T(8,128)S(1)}, s32[1,8,16]{2,1,0:T(8,128)}, bf16[1,8,16,128,128]{4,3,2,1,0:T(8,128)(2,1)}, s32[1,8,16]{2,1,0:T(...) while((s32[]{:T(128)}, f32[32,8,128]{2,0,1:T(8,128)S(1)}, ...), condition=%wide.region_2.3_spmd.clone, body=%wide.region_0.2_spmd.clone.sunk | while | flops 16975076 | bytes 2102115 | solution.py:34
  22.8 1.5 fusion.121
  29.4 1.5 fusion.121
  36.1 1.5 fusion.121
  42.7 1.5 fusion.121
  49.3 1.5 fusion.121
  55.9 1.5 fusion.121
  71.9 14.1 %all_gather.25 = bf16[128,1024]{1,0:T(8,128)(2,1)S(1)} all-gather(bf16[32,1024]{1,0:T(8,128)(2,1)S(1)} %copy_bitcast_fusion.7), channel_id=1, replica_groups=mesh['blk'=8,'feat'=4] {'feat'}, dimensions={0}, use_global_device_ids=true | all-gather | bytes 327680 | tf_op jit(solution)/shard_map/all_gather | solution.py:83
  87.0 24.1 %all-gather.3.cloned.1.call-done = bf16[64,8192]{1,0:T(8,128)(2,1)} async-done(((bf16[64,1024]{1,0:T(8,128)(2,1)}), bf16[64,8192]{1,0:T(8,128)(2,1)}) %all-gather.3.cloned.1.call-update) | async-done | bytes 1048592 | tf_op jit(solution)/shard_map/all_gather | solution.py:45
  111.2 62.0 %while.65 = (s32[]{:T(128)}, f32[64,8,128]{2,0,1:T(8,128)S(1)}, s32[1,8,16]{2,1,0:T(8,128)}, bf16[1,8,16,128,128]{4,3,2,1,0:T(8,128)(2,1)}, bf16[64,8192]{1,0:T(...) while((s32[]{:T(128)}, f32[64,8,128]{2,0,1:T(8,128)S(1)}, ...), condition=%wide.region_5.7_spmd.clone, body=%wide.region_3.0_spmd.clone.sunk | while | flops 33948852 | bytes 3674915 | solution.py:34
  116.1 1.5 fusion.125
  123.8 1.5 fusion.125
  131.6 1.5 fusion.125
  139.3 1.5 fusion.125
  147.1 1.5 fusion.125
  154.8 1.5 fusion.125
  162.6 1.5 fusion.125
  170.3 1.5 fusion.125
  173.2 16.0 %all_gather.27 = bf16[256,1024]{1,0:T(8,128)(2,1)S(1)} all-gather(bf16[64,1024]{1,0:T(8,128)(2,1)S(1)} %copy_bitcast_fusion.4), channel_id=1, replica_groups=mesh['blk'=8,'feat'=4] {'feat'}, dimensions={0}, use_global_device_ids=true | all-gather | bytes 655360 | tf_op jit(solution)/shard_map/all_gather | solution.py:83
  190.3 24.0 %all-gather.5.cloned.1.call-done = bf16[64,8192]{1,0:T(8,128)(2,1)} async-done(((bf16[64,1024]{1,0:T(8,128)(2,1)}), bf16[64,8192]{1,0:T(8,128)(2,1)}) %all-gather.5.cloned.1.call-update) | async-done | bytes 1048592 | tf_op jit(solution)/shard_map/all_gather | solution.py:45
  214.3 62.0 %while.66 = (s32[]{:T(128)}, f32[64,8,128]{2,0,1:T(8,128)S(1)}, s32[1,8,16]{2,1,0:T(8,128)}, bf16[1,8,16,128,128]{4,3,2,1,0:T(8,128)(2,1)}, bf16[64,8192]{1,0:T(...) while((s32[]{:T(128)}, f32[64,8,128]{2,0,1:T(8,128)S(1)}, ...), condition=%wide.region_8.10_spmd.clone, body=%wide.region_6.9_spmd.clone.sunk | while | flops 33948852 | bytes 3674915 | solution.py:34
  219.2 1.5 fusion.129
  227.0 1.5 fusion.129
  234.7 1.5 fusion.129
  242.4 1.5 fusion.129
  250.2 1.5 fusion.129
  257.9 1.5 fusion.129
  265.7 1.5 fusion.129
  273.4 1.5 fusion.129
  276.4 16.0 %all_gather.29 = bf16[256,1024]{1,0:T(8,128)(2,1)S(1)} all-gather(bf16[64,1024]{1,0:T(8,128)(2,1)S(1)} %copy_bitcast_fusion.3), channel_id=1, replica_groups=mesh['blk'=8,'feat'=4] {'feat'}, dimensions={0}, use_global_device_ids=true | all-gather | bytes 655360 | tf_op jit(solution)/shard_map/all_gather | solution.py:92
  294.1 75.5 %while.67 = (s32[]{:T(128)}, bf16[8,64,1024]{2,1,0:T(8,128)(2,1)S(1)}, s32[8]{0:T(128)S(1)}, s32[1,8,16]{2,1,0:T(8,128)}, bf16[1,8,16,128,128]{4,3,2,1,0:T(8,128...) while((s32[]{:T(128)}, ...), condition=%wide.region_17.19_spmd.clone, body=%wide.region_15.18_spmd.clone.sunk | while | flops 33948852 | bytes 4592431 | solution.py:67
  370.7 36.5 %reduce-scatter.3.cloned.1.call-done = bf16[1,64,1024]{2,1,0:T(8,128)(2,1)} async-done(((bf16[8,64,1024]{2,1,0:T(8,128)(2,1)}), bf16[1,64,1024]{2,1,0:T(8,128)(2,1)}) %reduce-scatter.3.cloned.1.call-update) | async-done | bytes 131088 | tf_op jit(solution)/shard_map/reduce_scatter | solution.py:66
  408.2 15.4 %all_gather.30 = bf16[256,1024]{1,0:T(8,128)(2,1)S(1)} all-gather(bf16[64,1024]{1,0:T(8,128)(2,1)S(1)} %fusion.75), channel_id=1, replica_groups=mesh['blk'=8,'feat'=4] {'feat'}, dimensions={0}, use_global_device_ids=true | all-gather | bytes 655360 | tf_op jit(solution)/shard_map/all_gather | solution.py:117
  424.0 80.9 %while.68 = (s32[]{:T(128)}, bf16[8,64,1024]{2,1,0:T(8,128)(2,1)S(1)}, s32[8]{0:T(128)S(1)}, s32[1,8,16]{2,1,0:T(8,128)}, bf16[1,8,16,128,128]{4,3,2,1,0:T(8,128...) while((s32[]{:T(128)}, ...), condition=%wide.region_21.23_spmd.clone, body=%wide.region_19.22_spmd.clone.sunk | while | flops 33948852 | bytes 4592743 | solution.py:67
  432.3 1.5 scatter_fusion.4
  442.4 1.5 scatter_fusion.4
  452.5 1.5 scatter_fusion.4
  462.7 1.5 scatter_fusion.4
  472.8 1.5 scatter_fusion.4
  482.9 1.5 scatter_fusion.4
  493.0 1.5 scatter_fusion.4
  503.1 1.5 scatter_fusion.4
  508.3 34.5 %reduce-scatter.5.cloned.1.call-done = bf16[1,64,1024]{2,1,0:T(8,128)(2,1)} async-done(((bf16[8,64,1024]{2,1,0:T(8,128)(2,1)}), bf16[1,64,1024]{2,1,0:T(8,128)(2,1)}) %reduce-scatter.5.cloned.1.call-update) | async-done | bytes 131088 | tf_op jit(solution)/shard_map/reduce_scatter | solution.py:66
  543.7 15.4 %all_gather.31 = bf16[256,1024]{1,0:T(8,128)(2,1)S(1)} all-gather(bf16[64,1024]{1,0:T(8,128)(2,1)S(1)} %fusion.73), channel_id=1, replica_groups=mesh['blk'=8,'feat'=4] {'feat'}, dimensions={0}, use_global_device_ids=true | all-gather | bytes 655360 | tf_op jit(solution)/shard_map/all_gather | solution.py:117
  559.4 24.2 %all-reduce.5 = (f32[]{:T(128)}, f32[]{:T(128)}, f32[32,256]{1,0:T(8,128)}, f32[64,172]{1,0:T(8,128)}) all-reduce(f32[]{:T(128)} %get-tuple-element.640, f32[]{:T(128)} %get-tuple-element.639, f32[32,256]{1,0:T(8,128)S(1)} %fusion.88, f32[64,172]{1,0:T(8,128)S(1)} %fusion.90), channel_id=1, replica_groups=mesh['blk'=8,'feat'=4] {'blk'}, use_global_device_ids=true, to_apply=%region_12.14 | all-reduce | flops 19202 | bytes 153616 | tf_op jit(solution)/shard_map/psum | solution.py:157
  584.8 14.6 %all-reduce.4.cloned.1.call-done = f32[64,256]{1,0:T(8,128)} async-done(((f32[64,256]{1,0:T(8,128)}), f32[64,256]{1,0:T(8,128)}) %all-reduce.4.cloned.1.call-update) | async-done | bytes 65552 | tf_op jit(solution)/shard_map/psum | solution.py:175
  599.4 1.5 copy.108
  (436 shorter events, 265.5 us)
Async XLA Ops:
  7.2 182.1 %copy-start = (bf16[256,256]{1,0:T(8,128)(2,1)S(1)}, bf16[256,256]{1,0:T(8,128)(2,1)}, u32[]{:S(2)}) copy-start(bf16[256,256]{1,0:T(8,128)(2,1)} %param.24) | copy-start | bytes 393220
  7.2 104.0 %all-gather.3.cloned.1.call-start = ((), (), s32[]{:S(2)}) async-start(), calls=%async_computation.2 | async-start | bytes 1179648 | tf_op jit(solution)/shard_map/all_gather | solution.py:45
  18.9 67.1 %copy-start.6 = (bf16[128,256]{1,0:T(8,128)(2,1)S(1)}, bf16[128,256]{1,0:T(8,128)(2,1)}, u32[]{:S(2)}) copy-start(bf16[128,256]{1,0:T(8,128)(2,1)} %param.23) | copy-start | bytes 196612
  87.0 127.3 %all-gather.5.cloned.1.call-start = ((), (), s32[]{:S(2)}) async-start(), calls=%async_computation.3 | async-start | bytes 1179648 | tf_op jit(solution)/shard_map/all_gather | solution.py:45
  111.2 79.1 %copy-start.7 = (s32[1024]{0:T(1024)S(1)}, s32[1024]{0:T(1024)}, u32[]{:S(2)}) copy-start(s32[1024]{0:T(1024)} %param.31) | copy-start | bytes 12292
  190.3 217.0 %reduce-scatter.3.cloned.1.call-start = ((), (), s32[]{:S(2)}) async-start(), calls=%async_computation.4 | async-start | bytes 1179648 | tf_op jit(solution)/shard_map/reduce_scatter | solution.py:66
  214.3 78.1 %copy-start.4 = (bf16[256,172]{0,1:T(8,128)(2,1)S(1)}, bf16[256,172]{0,1:T(8,128)(2,1)}, u32[]{:S(2)}) copy-start(bf16[256,172]{0,1:T(8,128)(2,1)} %param.25) | copy-start | bytes 264196
  214.3 78.1 %copy-start.5 = (s32[1024]{0:T(1024)S(1)}, s32[1024]{0:T(1024)}, u32[]{:S(2)}) copy-start(s32[1024]{0:T(1024)} %param.30) | copy-start | bytes 12292
  292.7 1.2 copy-start.3
  369.6 1.0 copy-start.1
  370.6 172.1 %reduce-scatter.5.cloned.1.call-start = ((), (), s32[]{:S(2)}) async-start(), calls=%async_computation.5 | async-start | bytes 1179648 | tf_op jit(solution)/shard_map/reduce_scatter | solution.py:66
  424.0 3.8 copy-start.8
  432.3 1.8 copy-start.9
  434.1 3.8 copy-start.8
  442.4 1.8 copy-start.9
  444.2 3.8 copy-start.8
  452.5 1.8 copy-start.9
  454.3 3.8 copy-start.8
  462.6 1.8 copy-start.9
  464.4 3.8 copy-start.8
  472.7 1.8 copy-start.9
  474.5 3.8 copy-start.8
  482.8 1.8 copy-start.9
  484.6 3.8 copy-start.8
  492.9 1.8 copy-start.9
  494.7 3.8 copy-start.8
  503.1 1.8 copy-start.9
  504.8 1.0 copy-start.2
  505.8 93.6 %all-reduce.4.cloned.1.call-start = ((), (), s32[]{:S(2)}) async-start(), calls=%async_computation.6 | async-start | bytes 131072 | tf_op jit(solution)/shard_map/psum | solution.py:175
Sparse Core Ops, SparseCore 0:
  87.1 24.0 all-gather.2
  190.4 23.8 all-gather.4
  370.8 36.4 reduce-scatter.2
  506.0 36.7 reduce-scatter.4
  546.2 53.1 all-reduce.3
where the time goes:
time: 615 us; the launch traced here: 609 us
  other arithmetic  142 us (23%)
  waiting for transfers between devices  134 us (22%)
  blocking collectives  113 us (18%)
  local copies, waits for them, and re-layouts  106 us (17%)
  matrix products  63.7 us (10%)
  loops' own time  33.6 us (5%)
  between operations  16.4 us (3%)
    reduce_scatter x2, waiting for transfers between devices, spread_back(): lax.psum_scatter(lax.map(term_one_panel, jnp.arange(lax.axis_size('blk')...  71 us
    all_gather x2, waiting for transfers between devices, hidden_aggregate(): lax.all_gather(table, 'blk', axis=1, tiled=True)  48.1 us
    dot_general x24, matrix products, folding_one_panel(): jnp.einsum('fsj,sij->fsi', chosen, values[0, turn_index], preferred_eleme...  36.4 us
    another operation x2, loops' own time, spread_back(): lax.map(term_one_panel, jnp.arange(lax.axis_size('blk') * 1, dtype=jnp.in...  32.5 us
    scatter-add x24, other arithmetic, folding_one_panel(): accumulated.at[:, targets[0, turn_index]]  31.2 us
    all_gather x2, blocking collectives, weight_columns(): lax.all_gather(gated, 'feat', axis=0, tiled=True)  30.8 us
    all_gather x2, blocking collectives, mix_features(): lax.all_gather(table, 'feat', axis=0, tiled=True)  30.1 us
    dynamic_slice x24, local copies, waits for them, and re-layouts, folding_one_panel(): live_slots = (slot_index < live_count[0, turn_index]).astype(jnp.float32)  29.8 us
  transfers between devices with their start and end apart: 5, of which 5 were waited for; matrix products, arithmetic and copies ran while one was open for 1% of the time, Pallas kernels for 0%

commit v1 on v0

--- a/solution.py
+++ b/solution.py
@@ -2,6 +2,27 @@
 import jax.numpy as jnp
 from jax import lax
 from jax.sharding import PartitionSpec as P
+
+
+def gather_around(value, axis, dim):
+    devices, here, span = (lax.axis_size(axis), lax.axis_index(axis), value.shape[dim])
+    right = [(i, (i + 1) % devices) for i in range(devices)]
+    left = [(i, (i - 1) % devices) for i in range(devices)]
+    out = jnp.zeros((*value.shape[:dim], devices * span, *value.shape[dim + 1 :]), value.dtype)
+    out = lax.dynamic_update_slice_in_dim(out, value, here * span, axis=dim)
+    from_left = from_right = value
+    middle = devices // 2
+    for hop in range(1, middle + 1):
+        from_left = lax.ppermute(from_left, axis, right)
+        out = lax.dynamic_update_slice_in_dim(
+            out, from_left, (here - hop) % devices * span, axis=dim
+        )
+        if hop < devices - middle:
+            from_right = lax.ppermute(from_right, axis, left)
+            out = lax.dynamic_update_slice_in_dim(
+                out, from_right, (here + hop) % devices * span, axis=dim
+            )
+    return out
 
 
 def elu(values):
@@ -42,7 +63,7 @@
     row_blocks = panel_rows // block_size
     folding = panel_folder(values, targets, sources, live_count, breadth, row_blocks, block_size)
     initial = jnp.zeros((breadth, row_blocks, block_size), jnp.float32)
-    summed = folding(initial, lax.all_gather(table, "blk", axis=1, tiled=True), jnp.int32(0))
+    summed = folding(initial, gather_around(table, "blk", 1), jnp.int32(0))
     return summed.reshape(breadth, panel_rows).astype(jnp.bfloat16)
 
 

time: 615 us -> 595 us (0.967)
  waiting for transfers between devices: 134 us -> 113 us
  starting transfers between devices: 0.2 us -> 16.2 us
  local copies, waits for them, and re-layouts: 106 us -> 97.3 us
    all_gather x2 -> x0, waiting for transfers between devices: 48.1 us -> none  [hidden_aggregate(): lax.all_gather(table, 'blk', axis=1, tiled=True)]
    ppermute x0 -> x14, waiting for transfers between devices: none -> 28.8 us  [the longest x8 28.8 us: gather_around(): from_left = lax.ppermute(from_left, axis, right)]
    ppermute x0 -> x14, starting transfers between devices: none -> 16.1 us  [the longest x6 15.9 us: gather_around(): from_right = lax.ppermute(from_right, axis, left)]
    reshape x24, local copies, waits for them, and re-layouts: 15.1 us -> 0.63 us  [folding_one_panel(): window = window.reshape(breadth, row_blocks, block_size)]
  transfers between devices with their start and end apart: 5 -> 17, of which waited for: 5 -> 11; matrix products, arithmetic and copies ran while one was open for 1% -> 1% of each run, Pallas kernels for 0% -> 0%
where the time goes in v1:
time: 595 us; the launch traced here: 589 us
  other arithmetic  137 us (23%)
  blocking collectives  113 us (19%)
  waiting for transfers between devices  113 us (19%)
  local copies, waits for them, and re-layouts  97.3 us (16%)
  matrix products  62.4 us (10%)
  loops' own time  33.4 us (6%)
  between operations  16.6 us (3%)
  starting transfers between devices  16.2 us (3%)
    reduce_scatter x2, waiting for transfers between devices, spread_back(): lax.psum_scatter(lax.map(term_one_panel, jnp.arange(lax.axis_size('blk')...  69.4 us
    dot_general x24, matrix products, folding_one_panel(): jnp.einsum('fsj,sij->fsi', chosen, values[0, turn_index], preferred_eleme...  36.3 us
    another operation x2, loops' own time, spread_back(): lax.map(term_one_panel, jnp.arange(lax.axis_size('blk') * 1, dtype=jnp.in...  32.2 us
    scatter-add x24, other arithmetic, folding_one_panel(): accumulated.at[:, targets[0, turn_index]]  31.2 us
    all_gather x2, blocking collectives, weight_columns(): lax.all_gather(gated, 'feat', axis=0, tiled=True)  30.7 us
    all_gather x2, blocking collectives, mix_features(): lax.all_gather(table, 'feat', axis=0, tiled=True)  30.2 us
    dynamic_slice x24, local copies, waits for them, and re-layouts, folding_one_panel(): live_slots = (slot_index < live_count[0, turn_index]).astype(jnp.float32)  29.8 us
    ppermute x8, waiting for transfers between devices, gather_around(): from_left = lax.ppermute(from_left, axis, right)  28.8 us
  transfers between devices with their start and end apart: 17, of which 11 were waited for; matrix products, arithmetic and copies ran while one was open for 1% of the time, Pallas kernels for 0%

profile of v1, /device:TPU:0, one launch (start us, length us, event | category | flops | bytes accessed | tf_op | source)
XLA Modules:
  0.0 588.9 jit_solution(5558316345303115906)
XLA Ops:
  7.2 11.6 %all_gather.18 = bf16[32,8192]{1,0:T(8,128)(2,1)S(1)} all-gather(bf16[32,1024]{1,0:T(8,128)(2,1)} %param.22), channel_id=1, replica_groups=mesh['blk'=8,'feat'=4] {'blk'}, dimensions={1}, use_global_device_ids=true | all-gather | bytes 589824 | tf_op jit(solution)/shard_map/all_gather | solution.py:162
  18.9 52.9 %while.64 = (s32[]{:T(128)}, f32[32,8,128]{2,0,1:T(8,128)S(1)}, s32[1,8,16]{2,1,0:T(8,128)}, bf16[1,8,16,128,128]{4,3,2,1,0:T(8,128)(2,1)}, s32[1,8,16]{2,1,0:T(...) while((s32[]{:T(128)}, f32[32,8,128]{2,0,1:T(8,128)S(1)}, ...), condition=%wide.region_2.3_spmd.clone, body=%wide.region_0.2_spmd.clone.sunk | while | flops 16975076 | bytes 2102615 | solution.py:55
  22.8 1.5 fusion.123
  29.4 1.5 fusion.123
  71.9 14.1 %all_gather.19 = bf16[128,1024]{1,0:T(8,128)(2,1)S(1)} all-gather(bf16[32,1024]{1,0:T(8,128)(2,1)S(1)} %copy_bitcast_fusion.7), channel_id=1, replica_groups=mesh['blk'=8,'feat'=4] {'feat'}, dimensions={0}, use_global_device_ids=true | all-gather | bytes 327680 | tf_op jit(solution)/shard_map/all_gather | solution.py:104
  86.5 2.6 collective-permute-start.1
  89.1 3.2 collective-permute-done
  92.3 2.6 collective-permute-start.3
  95.0 4.0 collective-permute-done.2
  98.9 2.6 collective-permute-start.5
  101.6 3.5 collective-permute-done.4
  105.1 5.2 collective-permute-done.6
  110.4 54.8 %while.65 = (s32[]{:T(128)}, f32[64,8,128]{2,0,1:T(8,128)S(1)}, s32[1,8,16]{2,1,0:T(8,128)}, bf16[1,8,16,128,128]{4,3,2,1,0:T(8,128)(2,1)}, bf16[64,8192]{1,0:T(...) while((s32[]{:T(128)}, f32[64,8,128]{2,0,1:T(8,128)S(1)}, ...), condition=%wide.region_5.7_spmd.clone, body=%wide.region_3.0_spmd.clone.sunk | while | flops 33948852 | bytes 3675415 | solution.py:55
  113.7 1.5 fusion.127
  120.5 1.5 fusion.127
  127.4 1.5 fusion.127
  134.2 1.5 fusion.127
  141.1 1.5 fusion.127
  147.9 1.5 fusion.127
  154.8 1.5 fusion.127
  161.6 1.5 fusion.127
  165.3 16.1 %all_gather.20 = bf16[256,1024]{1,0:T(8,128)(2,1)S(1)} all-gather(bf16[64,1024]{1,0:T(8,128)(2,1)S(1)} %copy_bitcast_fusion.4), channel_id=1, replica_groups=mesh['blk'=8,'feat'=4] {'feat'}, dimensions={0}, use_global_device_ids=true | all-gather | bytes 655360 | tf_op jit(solution)/shard_map/all_gather | solution.py:104
  181.9 2.6 collective-permute-start.8
  184.5 2.6 collective-permute-done.7
  187.2 2.7 collective-permute-start.10
  189.9 2.6 collective-permute-done.9
  192.5 2.7 collective-permute-start.12
  195.2 2.6 collective-permute-done.11
  197.8 5.2 collective-permute-done.13
  203.1 54.8 %while.66 = (s32[]{:T(128)}, f32[64,8,128]{2,0,1:T(8,128)S(1)}, s32[1,8,16]{2,1,0:T(8,128)}, bf16[1,8,16,128,128]{4,3,2,1,0:T(8,128)(2,1)}, bf16[64,8192]{1,0:T(...) while((s32[]{:T(128)}, f32[64,8,128]{2,0,1:T(8,128)S(1)}, ...), condition=%wide.region_8.10_spmd.clone, body=%wide.region_6.9_spmd.clone.sunk | while | flops 33948852 | bytes 3675415 | solution.py:55
  206.3 1.5 fusion.131
  213.2 1.5 fusion.131
  220.0 1.5 fusion.131
  226.9 1.5 fusion.131
  233.8 1.5 fusion.131
  240.6 1.5 fusion.131
  247.5 1.5 fusion.131
  254.3 1.5 fusion.131
  257.9 15.9 %all_gather.21 = bf16[256,1024]{1,0:T(8,128)(2,1)S(1)} all-gather(bf16[64,1024]{1,0:T(8,128)(2,1)S(1)} %copy_bitcast_fusion.3), channel_id=1, replica_groups=mesh['blk'=8,'feat'=4] {'feat'}, dimensions={0}, use_global_device_ids=true | all-gather | bytes 655360 | tf_op jit(solution)/shard_map/all_gather | solution.py:113
  275.4 75.5 %while.67 = (s32[]{:T(128)}, bf16[8,64,1024]{2,1,0:T(8,128)(2,1)S(1)}, s32[8]{0:T(128)S(1)}, s32[1,8,16]{2,1,0:T(8,128)}, bf16[1,8,16,128,128]{4,3,2,1,0:T(8,128...) while((s32[]{:T(128)}, ...), condition=%wide.region_17.19_spmd.clone, body=%wide.region_15.18_spmd.clone.sunk | while | flops 33948852 | bytes 4592423 | solution.py:88
  352.0 34.9 %reduce-scatter.3.cloned.1.call-done = bf16[1,64,1024]{2,1,0:T(8,128)(2,1)} async-done(((bf16[8,64,1024]{2,1,0:T(8,128)(2,1)}), bf16[1,64,1024]{2,1,0:T(8,128)(2,1)}) %reduce-scatter.3.cloned.1.call-update) | async-done | bytes 131088 | tf_op jit(solution)/shard_map/reduce_scatter | solution.py:87
  387.9 15.4 %all_gather.22 = bf16[256,1024]{1,0:T(8,128)(2,1)S(1)} all-gather(bf16[64,1024]{1,0:T(8,128)(2,1)S(1)} %fusion.75), channel_id=1, replica_groups=mesh['blk'=8,'feat'=4] {'feat'}, dimensions={0}, use_global_device_ids=true | all-gather | bytes 655360 | tf_op jit(solution)/shard_map/all_gather | solution.py:138
  404.2 80.8 %while.68 = (s32[]{:T(128)}, bf16[8,64,1024]{2,1,0:T(8,128)(2,1)S(1)}, s32[8]{0:T(128)}, s32[1,8,16]{2,1,0:T(8,128)}, bf16[1,8,16,128,128]{4,3,2,1,0:T(8,128)(2,...) while((s32[]{:T(128)}, ...), condition=%wide.region_21.23_spmd.clone, body=%wide.region_19.22_spmd.clone.sunk | while | flops 33948852 | bytes 4592423 | solution.py:88
  488.4 34.5 %reduce-scatter.5.cloned.1.call-done = bf16[1,64,1024]{2,1,0:T(8,128)(2,1)} async-done(((bf16[8,64,1024]{2,1,0:T(8,128)(2,1)}), bf16[1,64,1024]{2,1,0:T(8,128)(2,1)}) %reduce-scatter.5.cloned.1.call-update) | async-done | bytes 131088 | tf_op jit(solution)/shard_map/reduce_scatter | solution.py:87
  523.9 15.4 %all_gather.23 = bf16[256,1024]{1,0:T(8,128)(2,1)S(1)} all-gather(bf16[64,1024]{1,0:T(8,128)(2,1)S(1)} %fusion.73), channel_id=1, replica_groups=mesh['blk'=8,'feat'=4] {'feat'}, dimensions={0}, use_global_device_ids=true | all-gather | bytes 655360 | tf_op jit(solution)/shard_map/all_gather | solution.py:138
  539.5 24.1 %all-reduce.5 = (f32[]{:T(128)}, f32[]{:T(128)}, f32[32,256]{1,0:T(8,128)}, f32[64,172]{1,0:T(8,128)}) all-reduce(f32[]{:T(128)} %get-tuple-element.640, f32[]{:T(128)} %get-tuple-element.639, f32[32,256]{1,0:T(8,128)S(1)} %fusion.88, f32[64,172]{1,0:T(8,128)S(1)} %fusion.90), channel_id=1, replica_groups=mesh['blk'=8,'feat'=4] {'blk'}, use_global_device_ids=true, to_apply=%region_12.14 | all-reduce | flops 19202 | bytes 153616 | tf_op jit(solution)/shard_map/psum | solution.py:178
  565.0 14.8 %all-reduce.4.cloned.1.call-done = f32[64,256]{1,0:T(8,128)} async-done(((f32[64,256]{1,0:T(8,128)}), f32[64,256]{1,0:T(8,128)}) %all-reduce.4.cloned.1.call-update) | async-done | bytes 65552 | tf_op jit(solution)/shard_map/psum | solution.py:196
  579.8 1.5 copy.124
  (442 shorter events, 268.3 us)
Async XLA Ops:
  7.2 174.3 %copy-start = (bf16[256,256]{1,0:T(8,128)(2,1)S(1)}, bf16[256,256]{1,0:T(8,128)(2,1)}, u32[]{:S(2)}) copy-start(bf16[256,256]{1,0:T(8,128)(2,1)} %param.24) | copy-start | bytes 393220
  7.2 379.8 %reduce-scatter.3.cloned.1.call-start = ((), (), s32[]{:S(2)}) async-start(), calls=%async_computation.2 | async-start | bytes 1179648 | tf_op jit(solution)/shard_map/reduce_scatter | solution.py:87
  18.9 67.2 %copy-start.6 = (bf16[128,256]{1,0:T(8,128)(2,1)S(1)}, bf16[128,256]{1,0:T(8,128)(2,1)}, u32[]{:S(2)}) copy-start(bf16[128,256]{1,0:T(8,128)(2,1)} %param.23) | copy-start | bytes 196612
  86.4 5.9 collective-permute-start
  86.5 5.8 collective-permute-start.1
  92.3 6.6 %collective-permute-start.2 = (bf16[64,1024]{1,0:T(8,128)(2,1)S(1)}, bf16[64,1024]{1,0:T(8,128)(2,1)S(1)}, u32[]{:S(2)}, u32[]{:S(2)}) collective-permute-start(bf16[64,1024]{1,0:T(8,128)(2,1)S(1)} %collective-permute-done), channel_id=1, source_target_pairs={{0,4},{4,8},{8,12},{12,16},{16,20},{20,24},{24,28},{28,0},{1,5},{5... | collective-permute-start | bytes 393224 | tf_op jit(solution)/shard_map/ppermute | solution.py:16
  92.3 6.6 %collective-permute-start.3 = (bf16[64,1024]{1,0:T(8,128)(2,1)S(1)}, bf16[64,1024]{1,0:T(8,128)(2,1)S(1)}, u32[]{:S(2)}, u32[]{:S(2)}) collective-permute-start(bf16[64,1024]{1,0:T(8,128)(2,1)S(1)} %collective-permute-done.1), channel_id=1, source_target_pairs={{0,28},{4,0},{8,4},{12,8},{16,12},{20,16},{24,20},{28,24},{1,29},{... | collective-permute-start | bytes 393224 | tf_op jit(solution)/shard_map/ppermute | solution.py:21
  98.9 6.1 %collective-permute-start.4 = (bf16[64,1024]{1,0:T(8,128)(2,1)S(1)}, bf16[64,1024]{1,0:T(8,128)(2,1)S(1)}, u32[]{:S(2)}, u32[]{:S(2)}) collective-permute-start(bf16[64,1024]{1,0:T(8,128)(2,1)S(1)} %collective-permute-done.2), channel_id=1, source_target_pairs={{0,4},{4,8},{8,12},{12,16},{16,20},{20,24},{24,28},{28,0},{1,5},{5... | collective-permute-start | bytes 393224 | tf_op jit(solution)/shard_map/ppermute | solution.py:16
  98.9 6.2 %collective-permute-start.5 = (bf16[64,1024]{1,0:T(8,128)(2,1)S(1)}, bf16[64,1024]{1,0:T(8,128)(2,1)S(1)}, u32[]{:S(2)}, u32[]{:S(2)}) collective-permute-start(bf16[64,1024]{1,0:T(8,128)(2,1)S(1)} %collective-permute-done.3), channel_id=1, source_target_pairs={{0,28},{4,0},{8,4},{12,8},{16,12},{20,16},{24,20},{28,24},{1,29},{... | collective-permute-start | bytes 393224 | tf_op jit(solution)/shard_map/ppermute | solution.py:21
  105.1 5.3 collective-permute-start.6
  110.4 74.1 %copy-start.7 = (s32[1024]{0:T(1024)S(1)}, s32[1024]{0:T(1024)}, u32[]{:S(2)}) copy-start(s32[1024]{0:T(1024)} %param.31) | copy-start | bytes 12292
  181.8 5.3 collective-permute-start.7
  181.9 5.3 collective-permute-start.8
  187.1 5.3 collective-permute-start.9
  187.2 5.3 collective-permute-start.10
  192.4 5.3 collective-permute-start.11
  192.5 5.3 collective-permute-start.12
  197.7 5.3 collective-permute-start.13
  203.1 70.8 %copy-start.4 = (bf16[256,172]{0,1:T(8,128)(2,1)S(1)}, bf16[256,172]{0,1:T(8,128)(2,1)}, u32[]{:S(2)}) copy-start(bf16[256,172]{0,1:T(8,128)(2,1)} %param.25) | copy-start | bytes 264196
  203.1 70.8 %copy-start.5 = (s32[1024]{0:T(1024)S(1)}, s32[1024]{0:T(1024)}, u32[]{:S(2)}) copy-start(s32[1024]{0:T(1024)} %param.30) | copy-start | bytes 12292
  274.2 1.1 copy-start.3
  351.0 1.0 copy-start.1
  352.0 170.9 %reduce-scatter.5.cloned.1.call-start = ((), (), s32[]{:S(2)}) async-start(), calls=%async_computation.3 | async-start | bytes 1179648 | tf_op jit(solution)/shard_map/reduce_scatter | solution.py:87
  485.0 1.0 copy-start.2
  486.0 93.8 %all-reduce.4.cloned.1.call-start = ((), (), s32[]{:S(2)}) async-start(), calls=%async_computation.4 | async-start | bytes 131072 | tf_op jit(solution)/shard_map/psum | solution.py:196
Sparse Core Ops, SparseCore 0:
  352.1 34.8 reduce-scatter.2
  486.1 36.7 reduce-scatter.4
  526.5 53.1 all-reduce.3
